TPU v7x, 256 devices: a whole 4x4x8 slice. The times are simulated.
256 devices in a mesh: gz: 8 (over z_lo, core), gx: 32 (over x, z_hi, y).
Axes of the slice: x: 4, y: 4, z: 8 (z_hi: 2, z_lo: 4; z = z_hi * 4 + z_lo), core: 2. Of those that a mesh axis runs over, the one named last changes fastest.
Arguments:
- state: float32 [6, 128, 8192], P(None, 'gz', 'gx'), may hold values from -5 to 5, as said below
- state_cot: float32 [6, 128, 8192], P(None, 'gz', 'gx'), may hold values from -6 to 6
- w_in: bfloat16 [128, 12], replicated, may hold values from -1.75 to 1.75
- w_mid: bfloat16 [128, 128], replicated, may hold values from -0.5 to 0.5
- w_out: bfloat16 [6, 128], replicated, may hold values from -0.5 to 0.5
- radiation: float32 [128, 128], replicated, may hold values from -0.5 to 0.5
- fall_rate: float32 [8192], P('gx'), may hold values from 20 to 2000
- active: int32 [8192], P('gx'), may hold values 0 or 1
Outputs:
- new_state: float32 [6, 128, 8192], P(None, 'gz', 'gx')
- state_grad: float32 [6, 128, 8192], P(None, 'gz', 'gx')
- grad_in: float32 [128, 12], replicated
- grad_mid: float32 [128, 128], replicated
- grad_out: float32 [6, 128], replicated
Inputs may be any that keep to these rules, and one draw needn't show every extreme that they name: `state`: fields come in the order u, v, w, theta, total water, rain water; rain water lies between 0.05 and 1.
All inputs are finite; a program needn't handle non-finite values. No bound on the sum of `active` on one device may be relied on, other than what follows from the above.
Results may differ from a plain program's by a relative error of at most 0.00045.
The roundings to bfloat16 on the way count: a program that leaves them out, or rounds other values in their place, can miss the bound.
Values sent between devices are 32-bit elements; how exact they have to be, the bound alone decides.
No kernel may reach another device: no remote copies, remote signals or barrier semaphores. Data moves between devices by JAX's collectives and lax.ppermute only.
A program may use at most 64 MiB of HBM per device.

v0:
```python
import jax
import jax.numpy as jnp
from jax import lax
from jax.sharding import PartitionSpec as P

NY = 64
DIFFUSION = 0.1
TIME_STEP = 0.25
CLOSURE_GAIN = 1.0
HEATING_GAIN = 1.0
FALL_GAIN = 1.0


def prefix(shard, axis, combine, identity, reverse):
    length, index = (lax.axis_size(axis), lax.axis_index(axis))
    everything = jax.tree.map(lambda part: lax.all_gather(part, axis), shard)
    start = jax.tree.map(
        lambda part, zero: jnp.broadcast_to(jnp.asarray(zero, part.dtype), part.shape),
        shard,
        identity,
    )

    def step(k, before):
        at = length - 1 - k if reverse else k
        reached = at > index if reverse else at < index
        new = combine(before, jax.tree.map(lambda part: part[at], everything))
        return jax.tree.map(lambda a, b: jnp.where(reached, a, b), new, before)

    return lax.fori_loop(0, length, step, start)


def passed_along(shard, axis, by):
    length = lax.axis_size(axis)
    return lax.ppermute(shard, axis, [(i, (i + by) % length) for i in range(length)])


def padded_2(shard, sides, width):
    for axis, dim in sides:
        size, length = (lax.axis_size(axis), shard.shape[dim])
        up = [(i, (i + 1) % size) for i in range(size)]
        down = [(j, i) for i, j in up]
        last = lax.slice_in_dim(shard, length - width, length, axis=dim)
        first = lax.slice_in_dim(shard, 0, width, axis=dim)
        before = lax.ppermute(last, axis, up)
        after = lax.ppermute(first, axis, down)
        shard = jnp.concatenate([before, shard, after], axis=dim)
    return shard


def contract(left, right, left_dim, right_dim):
    return lax.dot_general(
        left, right, (((left_dim,), (right_dim,)), ((), ())), preferred_element_type=jnp.float32
    )


def mlp_forward(features, w_in, w_mid, w_out):
    hidden_one = jnp.tanh(jnp.dot(w_in, features, preferred_element_type=jnp.float32)).astype(
        jnp.bfloat16
    )
    hidden_two = jnp.tanh(jnp.dot(w_mid, hidden_one, preferred_element_type=jnp.float32)).astype(
        jnp.bfloat16
    )
    return jnp.dot(w_out, hidden_two, preferred_element_type=jnp.float32)


def mlp_backward(features, out_cot, w_in, w_mid, w_out):
    tanh_one = jnp.tanh(jnp.dot(w_in, features, preferred_element_type=jnp.float32))
    hidden_one = tanh_one.astype(jnp.bfloat16)
    tanh_two = jnp.tanh(jnp.dot(w_mid, hidden_one, preferred_element_type=jnp.float32))
    hidden_two = tanh_two.astype(jnp.bfloat16)
    term_out = contract(out_cot, hidden_two, 1, 1)
    pre_two = (contract(w_out, out_cot, 0, 0) * (1.0 - tanh_two * tanh_two)).astype(jnp.bfloat16)
    term_mid = contract(pre_two, hidden_one, 1, 1)
    pre_one = (contract(w_mid, pre_two, 0, 0) * (1.0 - tanh_one * tanh_one)).astype(jnp.bfloat16)
    term_in = contract(pre_one, features, 1, 1)
    feature_cot = contract(w_in, pre_one, 0, 0)
    return (feature_cot, (term_in, term_mid, term_out))


def interior(padded):
    return padded[..., 2 * NY : padded.shape[-1] - 2 * NY]


def dynamics(padded):
    columns = padded.shape[-1] - 4 * NY

    def along_x(offset):
        first_col = 2 * NY + offset * NY
        return padded[..., first_col : first_col + columns]

    center = along_x(0)
    y_place = jnp.arange(columns) % NY
    y_last = y_place == NY - 1
    y_first = y_place == 0
    y_plus = jnp.where(y_last, jnp.roll(center, NY - 1, -1), jnp.roll(center, -1, -1))
    y_minus = jnp.where(y_first, jnp.roll(center, 1 - NY, -1), jnp.roll(center, 1, -1))
    x_plus, x_minus = (along_x(1), along_x(-1))
    deriv_x = (8.0 * (x_plus - x_minus) - (along_x(2) - along_x(-2))) / 12.0
    deriv_y = (y_plus - y_minus) / 2.0
    laplace = x_plus + x_minus + y_plus + y_minus - 4.0 * center
    return (-(center[0] * deriv_x + center[1] * deriv_y) + DIFFUSION * laplace, deriv_x)


def compose(earlier, later):
    return (later[0] * earlier[0], later[1] + later[0] * earlier[1])


def running_maps(source, retained):
    factors = jnp.broadcast_to(retained, source.shape)
    return lax.associative_scan(compose, (factors, source), axis=0)


def sediment_forward(rain_water, fall_speed):
    fresh_share = 1.0 / (1.0 + fall_speed)
    retained = fall_speed / (1.0 + fall_speed)
    factors, values = running_maps(jnp.flip(fresh_share * rain_water, 0), retained)
    inflow = prefix(
        (factors[-1], values[-1]),
        "gz",
        compose,
        (jnp.ones_like(fall_speed), jnp.zeros_like(fall_speed)),
        True,
    )
    return jnp.flip(values + factors * inflow[1], 0)


def sediment_adjoint(source, fall_speed):
    fresh_share = 1.0 / (1.0 + fall_speed)
    retained = fall_speed / (1.0 + fall_speed)
    factors, values = running_maps(fresh_share * source, retained)
    inflow = prefix(
        (factors[-1], values[-1]),
        "gz",
        compose,
        (jnp.ones_like(fall_speed), jnp.zeros_like(fall_speed)),
        False,
    )
    return values + factors * inflow[1]


def heating(theta, radiation):
    levels = theta.shape[0]
    own_rows = lax.dynamic_slice_in_dim(radiation, lax.axis_index("gz") * levels, levels, 0)
    return jnp.dot(
        own_rows,
        lax.all_gather(theta, "gz", axis=0, tiled=True),
        precision=lax.Precision.HIGHEST,
        preferred_element_type=jnp.float32,
    )


def heating_adjoint(lead_theta, radiation):
    levels = lead_theta.shape[0]
    own_rows = lax.dynamic_slice_in_dim(radiation, lax.axis_index("gz") * levels, levels, 0)
    return lax.psum_scatter(
        lax.dot_general(
            own_rows,
            lead_theta,
            (((0,), (0,)), ((), ())),
            precision=lax.Precision.HIGHEST,
            preferred_element_type=jnp.float32,
        ),
        "gz",
        scatter_dimension=0,
        tiled=True,
    )


def tendency(padded, w_in, w_mid, w_out, radiation, fall_speed, live):
    moved, deriv_x = dynamics(padded)
    center = interior(padded)
    fields, levels, columns = center.shape
    features = (
        jnp.concatenate([center, deriv_x], 0)
        .astype(jnp.bfloat16)
        .reshape(2 * fields, levels * columns)
    )
    closure = mlp_forward(features, w_in, w_mid, w_out).reshape(fields, levels, columns)
    total = moved + CLOSURE_GAIN * closure
    total = total.at[3].add(HEATING_GAIN * heating(center[3], radiation))
    fallen = sediment_forward(center[5], fall_speed)
    return total.at[5].add(FALL_GAIN * live * (fallen - center[5]))


def adjoint_tendency(padded, lead, w_in, w_mid, w_out, radiation, fall_speed, live):
    outputs, pullback = jax.vjp(dynamics, padded)
    center = interior(padded)
    fields, levels, columns = center.shape
    features = (
        jnp.concatenate([center, outputs[1]], 0)
        .astype(jnp.bfloat16)
        .reshape(2 * fields, levels * columns)
    )
    out_cot = (CLOSURE_GAIN * lead).astype(jnp.bfloat16).reshape(fields, levels * columns)
    feature_cot, grads = mlp_backward(features, out_cot, w_in, w_mid, w_out)
    feature_cot = feature_cot.reshape(2 * fields, levels, columns)
    padded_cot = pullback((lead, feature_cot[fields:]))[0]
    rim_width = 2 * NY
    from_next = passed_along(padded_cot[..., :rim_width], "gx", -1)
    from_prev = passed_along(padded_cot[..., padded_cot.shape[-1] - rim_width :], "gx", 1)
    result = interior(padded_cot) + feature_cot[:fields]
    result = result.at[..., :rim_width].add(from_prev)
    result = result.at[..., columns - rim_width :].add(from_next)
    result = result.at[3].add(HEATING_GAIN * heating_adjoint(lead[3], radiation))
    masked = live * lead[5]
    return (result.at[5].add(FALL_GAIN * (sediment_adjoint(masked, fall_speed) - masked)), grads)


def on_device(state, state_cot, w_in, w_mid, w_out, radiation, fall_rate, active):
    live = active.astype(jnp.float32)

    def extend(fields):
        return padded_2(fields, (("gx", 2),), 2 * NY)

    def section_tendency(padded):
        return tendency(padded, w_in, w_mid, w_out, radiation, fall_rate, live)

    def section_adjoint(padded, lead):
        return adjoint_tendency(padded, lead, w_in, w_mid, w_out, radiation, fall_rate, live)

    padded_zero = extend(state)
    section_one = state + TIME_STEP * section_tendency(padded_zero)
    padded_one = extend(section_one)
    section_two = 0.75 * state + 0.25 * (section_one + TIME_STEP * section_tendency(padded_one))
    padded_two = extend(section_two)
    new_state = state / 3.0 + 2.0 / 3.0 * (section_two + TIME_STEP * section_tendency(padded_two))
    lead_two = 2.0 / 3.0 * state_cot
    grad_state = state_cot / 3.0
    back_two, grads_two = section_adjoint(padded_two, lead_two)
    cot_two = lead_two + TIME_STEP * back_two
    lead_one = 0.25 * cot_two
    grad_state = grad_state + 0.75 * cot_two
    back_one, grads_one = section_adjoint(padded_one, lead_one)
    cot_one = lead_one + TIME_STEP * back_one
    back_zero, grads_zero = section_adjoint(padded_zero, cot_one)
    grad_state = grad_state + cot_one + TIME_STEP * back_zero
    totals = lax.psum(
        (
            TIME_STEP * (grads_two[0] + grads_one[0] + grads_zero[0]),
            TIME_STEP * (grads_two[1] + grads_one[1] + grads_zero[1]),
            TIME_STEP * (grads_two[2] + grads_one[2] + grads_zero[2]),
        ),
        ("gz", "gx"),
    )
    return (new_state, grad_state, totals[0], totals[1], totals[2])


def solution(mesh):
    placed = (P(None, "gz", "gx"), P(None, "gz", "gx"), P(), P(), P(), P(), P("gx"), P("gx"))
    return jax.shard_map(
        on_device,
        mesh=mesh,
        in_specs=placed,
        out_specs=(P(None, "gz", "gx"), P(None, "gz", "gx"), P(), P(), P()),
        check_vma=False,
    )
```

profile of v0, /device:TPU:1, one launch (start us, length us, event | category | flops | bytes accessed | tf_op | source)
XLA Modules:
  0.0 674.6 jit_solution(1791743276329991955)
XLA Ops:
  8.1 12.5 %collective-permute-start = (f32[6,16,128]{2,1,0:T(8,128)S(1)}, f32[6,16,128]{2,1,0:T(8,128)S(1)}, u32[]{:S(2)}, u32[]{:S(2)}) collective-permute-start(f32[6,16,128]{2,1,0:T(8,128)S(1)} %get-tuple-element.1230), channel_id=1, source_target_pairs={{1,0},{2,1},{3,2},{4,3},{5,4},{6,5},{7,6},{8,7},{9,8},{10,9},{11,1... | collective-permute-start | bytes 147464 | tf_op jit(solution)/shard_map/ppermute | solution.py:45
  21.9 1.4 bitcast_multiply_fusion
  23.6 1.5 fusion.147
  25.2 1.5 fusion.146
  27.7 1.6 fusion.145
  30.5 11.1 %all-gather.3 = f32[8,1,256]{2,1,0:T(1,128)S(1)} all-gather(f32[1,1,256]{2,1,0:T(1,128)S(1)} %add_bitcast_fusion.6), channel_id=1, replica_groups=mesh['gz'=8,'gx'=32] {'gz'}, dimensions={0}, use_global_device_ids=true | all-gather | bytes 9216 | tf_op jit(solution)/shard_map/all_gather | solution.py:16
  41.6 8.7 %all-gather.4 = f32[8,1,256]{2,1,0:T(1,128)S(1)} all-gather(f32[1,1,256]{2,1,0:T(1,128)S(1)} %add_bitcast_fusion.5), channel_id=1, replica_groups=mesh['gz'=8,'gx'=32] {'gz'}, dimensions={0}, use_global_device_ids=true | all-gather | bytes 9216 | tf_op jit(solution)/shard_map/all_gather | solution.py:16
  51.5 14.0 %all-gather = f32[1,128,256]{2,1,0:T(8,128)S(1)} all-gather(f32[1,16,256]{2,1,0:T(8,128)S(1)} %slice-done), channel_id=2, replica_groups=mesh['gz'=8,'gx'=32] {'gz'}, dimensions={1}, use_global_device_ids=true | all-gather | bytes 147456 | tf_op jit(solution)/shard_map/all_gather | solution.py:146
  73.2 10.1 %all-gather.5 = f32[8,1,256]{2,1,0:T(1,128)S(1)} all-gather(f32[1,1,256]{2,1,0:T(1,128)S(1)} %add_bitcast_fusion.4), channel_id=1, replica_groups=mesh['gz'=8,'gx'=32] {'gz'}, dimensions={0}, use_global_device_ids=true | all-gather | bytes 9216 | tf_op jit(solution)/shard_map/all_gather | solution.py:16
  83.8 9.9 %collective-permute-start.2 = (f32[6,16,128]{2,1,0:T(8,128)S(1)}, f32[6,16,128]{2,1,0:T(8,128)S(1)}, u32[]{:S(2)}, u32[]{:S(2)}) collective-permute-start(f32[6,16,128]{2,1,0:T(8,128)S(1)} %get-tuple-element.1214), channel_id=1, source_target_pairs={{1,0},{2,1},{3,2},{4,3},{5,4},{6,5},{7,6},{8,7},{9,8},{10,9},{11,1... | collective-permute-start | bytes 147464 | tf_op jit(solution)/shard_map/ppermute | solution.py:45
  93.8 14.3 %all-gather.1 = f32[1,128,256]{2,1,0:T(8,128)S(1)} all-gather(f32[1,16,256]{2,1,0:T(8,128)S(1)} %get-tuple-element.1172), channel_id=3, replica_groups=mesh['gz'=8,'gx'=32] {'gz'}, dimensions={1}, use_global_device_ids=true | all-gather | bytes 147456 | tf_op jit(solution)/shard_map/all_gather | solution.py:146
  113.3 9.9 %collective-permute-start.4 = (f32[6,16,128]{2,1,0:T(8,128)S(1)}, f32[6,16,128]{2,1,0:T(8,128)S(1)}, u32[]{:S(2)}, u32[]{:S(2)}) collective-permute-start(f32[6,16,128]{2,1,0:T(8,128)S(1)} %get-tuple-element.1193), channel_id=1, source_target_pairs={{1,0},{2,1},{3,2},{4,3},{5,4},{6,5},{7,6},{8,7},{9,8},{10,9},{11,1... | collective-permute-start | bytes 147464 | tf_op jit(solution)/shard_map/ppermute | solution.py:45
  123.2 15.5 %all-gather.2 = f32[1,128,256]{2,1,0:T(8,128)} all-gather(f32[1,16,256]{2,1,0:T(8,128)S(1)} %get-tuple-element.1188), channel_id=4, replica_groups=mesh['gz'=8,'gx'=32] {'gz'}, dimensions={1}, use_global_device_ids=true | all-gather | bytes 147456 | tf_op jit(solution)/shard_map/all_gather | solution.py:146
  138.7 1.5 broadcast_multiply_fusion
  153.3 8.7 %all-gather.7 = f32[8,1,256]{2,1,0:T(1,128)S(1)} all-gather(f32[1,1,256]{2,1,0:T(1,128)S(1)} %add_bitcast_fusion.2), channel_id=1, replica_groups=mesh['gz'=8,'gx'=32] {'gz'}, dimensions={0}, use_global_device_ids=true | all-gather | bytes 9216 | tf_op jit(solution)/shard_map/all_gather | solution.py:16
  162.1 8.8 %while.111 = (s32[]{:T(128)}, f32[256]{0:T(256)}, s32[]{:T(128)}, f32[8,256]{1,0:T(8,128)S(1)}, f32[8,256]{1,0:T(8,128)S(1)}, /*index=5*/s32[]{:T(128)}, s32[]{:T(128)}) while((s32[]{:T(128)}, f32[256]{0:T(256)}, s32[]{:T(128)}, f32[8,256]{1,0:T(8,128)S(1)}, f32[8,256]{1,0:T(8,128)S(1)}, /*index=5*/s32[]{:T(128)}, ...), condition=%wide.region_10.11_spmd.clone, body=%wide.region_9.10_spmd.clone.sunk | while | flops 1028 | bytes 8301 | solution.py:29
  170.9 9.9 %collective-permute-start.7 = (f32[6,16,128]{2,1,0:T(8,128)S(1)}, f32[6,16,128]{2,1,0:T(8,128)S(1)}, u32[]{:S(2)}, u32[]{:S(2)}) collective-permute-start(f32[6,16,128]{2,1,0:T(8,128)S(1)} %get-tuple-element.1127), channel_id=1, source_target_pairs={{0,31},{1,0},{2,1},{3,2},{4,3},{5,4},{6,5},{7,6},{8,7},{9,8},{10,9... | collective-permute-start | bytes 147464 | tf_op jit(solution)/shard_map/ppermute | solution.py:34
  180.9 11.1 %collective-permute-done.6 = f32[6,16,128]{2,1,0:T(8,128)S(1)} collective-permute-done((f32[6,16,128]{2,1,0:T(8,128)S(1)}, f32[6,16,128]{2,1,0:T(8,128)S(1)}, u32[]{:S(2)}, u32[]{:S(2)}) %collective-permute-start.6) | collective-permute-done | bytes 49184 | tf_op jit(solution)/shard_map/ppermute | solution.py:34
  192.0 12.1 %reduce-scatter.4.cloned.1.call-done = f32[16,256]{1,0:T(8,128)} async-done(((f32[128,256]{1,0:T(8,128)}), f32[16,256]{1,0:T(8,128)}) %reduce-scatter.4.cloned.1.call-update) | async-done | bytes 16400 | tf_op jit(solution)/shard_map/reduce_scatter | solution.py:155
  211.1 2.2 fusion.2
  218.2 1.8 pad.467
  220.1 1.9 pad.468
  221.9 1.3 add.1082
  225.2 1.9 pad.470
  227.0 1.3 add.1084
  230.4 1.9 pad.472
  233.0 12.0 %all-gather.8 = f32[8,1,256]{2,1,0:T(1,128)S(1)} all-gather(f32[1,1,256]{2,1,0:T(1,128)S(1)} %add_bitcast_fusion.1), channel_id=1, replica_groups=mesh['gz'=8,'gx'=32] {'gz'}, dimensions={0}, use_global_device_ids=true | all-gather | bytes 9216 | tf_op jit(solution)/shard_map/all_gather | solution.py:16
  245.6 15.3 %while.112 = (s32[]{:T(128)}, f32[256]{0:T(256)}, s32[]{:T(128)}, f32[8,256]{1,0:T(8,128)}, f32[8,256]{1,0:T(8,128)}, /*index=5*/s32[]{:T(128)}, s32[]{:T(128)}) while((s32[]{:T(128)}, f32[256]{0:T(256)}, s32[]{:T(128)}, f32[8,256]{1,0:T(8,128)}, f32[8,256]{1,0:T(8,128)}, /*index=5*/s32[]{:T(128)}, s32[]{:T(128)}) %tuple.457), condition=%wide.region_15.16_spmd.clone, body=%wide.region_14.15_spmd.clone.sunk | while | flops 1028 | bytes 8301 | solution.py:29
  260.9 2.6 convolution_add_fusion.5
  263.5 2.4 convolution_add_fusion.1
  266.9 7.8 %collective-permute-start.9 = (f32[6,16,128]{2,1,0:T(8,128)}, f32[6,16,128]{2,1,0:T(8,128)S(1)}, u32[]{:S(2)}, u32[]{:S(2)}) collective-permute-start(f32[6,16,128]{2,1,0:T(8,128)} %get-tuple-element.1125), channel_id=1, source_target_pairs={{0,31},{1,0},{2,1},{3,2},{4,3},{5,4},{6,5},{7,6},{8,7},{9,8},{10,9... | collective-permute-start | bytes 147464 | tf_op jit(solution)/shard_map/ppermute | solution.py:34
  275.7 10.3 %collective-permute-done.8 = f32[6,16,128]{2,1,0:T(8,128)S(1)} collective-permute-done((f32[6,16,128]{2,1,0:T(8,128)}, f32[6,16,128]{2,1,0:T(8,128)S(1)}, u32[]{:S(2)}, u32[]{:S(2)}) %collective-permute-start.8) | collective-permute-done | bytes 49184 | tf_op jit(solution)/shard_map/ppermute | solution.py:34
  286.1 12.3 %reduce-scatter.6.cloned.1.call-done = f32[16,256]{1,0:T(8,128)} async-done(((f32[128,256]{1,0:T(8,128)}), f32[16,256]{1,0:T(8,128)}) %reduce-scatter.6.cloned.1.call-update) | async-done | bytes 16400 | tf_op jit(solution)/shard_map/reduce_scatter | solution.py:155
  299.9 1.6 multiply_reduce_fusion.1
  328.3 1.3 add.1046
  330.2 1.3 fusion.92
  332.1 1.3 pad_maximum_fusion.19
  334.2 1.9 pad.495
  336.8 12.1 %all-gather.9 = f32[8,1,256]{2,1,0:T(1,128)S(1)} all-gather(f32[1,1,256]{2,1,0:T(1,128)S(1)} %add_bitcast_fusion), channel_id=1, replica_groups=mesh['gz'=8,'gx'=32] {'gz'}, dimensions={0}, use_global_device_ids=true | all-gather | bytes 9216 | tf_op jit(solution)/shard_map/all_gather | solution.py:16
  349.4 14.0 %while.113 = (s32[]{:T(128)}, f32[256]{0:T(256)}, s32[]{:T(128)}, f32[8,256]{1,0:T(8,128)}, f32[8,256]{1,0:T(8,128)}, /*index=5*/s32[]{:T(128)}, s32[]{:T(128)}) while((s32[]{:T(128)}, f32[256]{0:T(256)}, s32[]{:T(128)}, f32[8,256]{1,0:T(8,128)}, f32[8,256]{1,0:T(8,128)}, /*index=5*/s32[]{:T(128)}, s32[]{:T(128)}) %tuple.458), condition=%wide.region_20.21_spmd.clone, body=%wide.region_19.20_spmd.clone.sunk | while | flops 1028 | bytes 8301 | solution.py:29
  364.2 10.4 %all-gather.6 = f32[8,1,256]{2,1,0:T(1,128)S(1)} all-gather(f32[1,1,256]{2,1,0:T(1,128)S(1)} %add_bitcast_fusion.3), channel_id=1, replica_groups=mesh['gz'=8,'gx'=32] {'gz'}, dimensions={0}, use_global_device_ids=true | all-gather | bytes 9216 | tf_op jit(solution)/shard_map/all_gather | solution.py:16
  375.1 14.2 %while.110 = (s32[]{:T(128)}, f32[256]{0:T(256)}, s32[]{:T(128)}, f32[8,256]{1,0:T(8,128)}, f32[8,256]{1,0:T(8,128)}, /*index=5*/s32[]{:T(128)}, s32[]{:T(128)}, s32[]{:T(128)}, s32[]{:T(128)}) while((s32[]{:T(128)}, f32[256]{0:T(256)}, s32[]{:T(128)}, f32[8,256]{1,0:T(8,128)}, f32[8,256]{1,0:T(8,128)}, /*index=5*/s32[]{:T(128)}, ...), condition=%wide.region_5.6_spmd.clone, body=%wide.region_4.5_spmd.clone.sunk | while | flops 1032 | bytes 8363 | solution.py:29
  389.5 1.8 fusion.14
  391.5 2.5 fusion.6
  395.7 8.6 %collective-permute-start.11 = (f32[6,16,128]{2,1,0:T(8,128)S(1)}, f32[6,16,128]{2,1,0:T(8,128)S(1)}, u32[]{:S(2)}, u32[]{:S(2)}) collective-permute-start(f32[6,16,128]{2,1,0:T(8,128)S(1)} %copy-done.103), channel_id=1, source_target_pairs={{0,31},{1,0},{2,1},{3,2},{4,3},{5,4},{6,5},{7,6},{8,7},{9,8},{10,9... | collective-permute-start | bytes 147464 | tf_op jit(solution)/shard_map/ppermute | solution.py:34
  404.7 73.1 %all-reduce.101 = (f32[128,12]{0,1:T(8,128)}, f32[6,128]{1,0:T(8,128)}) all-reduce(f32[128,12]{0,1:T(8,128)S(1)} %fusion.13, f32[6,128]{1,0:T(8,128)S(1)} %copy-done.124), channel_id=1, replica_groups=mesh['gz'=8,'gx'=32] {'gz','gx'}, use_global_device_ids=true, to_apply=%region_21.22 | all-reduce | flops 2304 | bytes 18432 | tf_op jit(solution)/shard_map/psum | solution.py:237
  480.0 186.6 %all-reduce.104.cloned.1.call-done = f32[128,128]{1,0:T(8,128)} async-done(((f32[128,128]{1,0:T(8,128)}), f32[128,128]{1,0:T(8,128)}) %all-reduce.104.cloned.1.call-update) | async-done | bytes 65552 | tf_op jit(solution)/shard_map/psum | solution.py:237
  666.6 1.5 copy.127
  (725 shorter events, 139.6 us)
Async XLA Ops:
  7.2 62.3 %copy-start = (f32[128,128]{1,0:T(8,128)S(1)}, f32[128,128]{1,0:T(8,128)}, u32[]{:S(2)}) copy-start(f32[128,128]{1,0:T(8,128)} %param.61) | copy-start | bytes 196612
  7.2 44.3 %slice-start = ((f32[6,16,256]{2,1,0:T(8,128)}), f32[1,16,256]{2,1,0:T(8,128)S(1)}, s32[]{:S(2)}) async-start(f32[6,16,256]{2,1,0:T(8,128)} %param.56), calls=%async_computation.7 | async-start | bytes 32768 | tf_op jit(solution)/shard_map/slice | solution.py:180
  7.2 58.3 %copy-start.8 = (f32[6,16,256]{2,1,0:T(8,128)S(1)}, f32[6,16,256]{2,1,0:T(8,128)}, u32[]{:S(2)}) copy-start(f32[6,16,256]{2,1,0:T(8,128)} %param.56) | copy-start | bytes 294916
  7.2 58.5 %copy-start.63 = (bf16[128,12]{0,1:T(8,128)(2,1)S(1)}, bf16[128,12]{0,1:T(8,128)(2,1)}, u32[]{:S(2)}) copy-start(bf16[128,12]{0,1:T(8,128)(2,1)} %param.58) | copy-start | bytes 9220
  7.2 196.9 %reduce-scatter.4.cloned.1.call-start = ((), (), s32[]{:S(2)}) async-start(), calls=%async_computation.3 | async-start | bytes 147456 | tf_op jit(solution)/shard_map/reduce_scatter | solution.py:155
  8.1 57.4 %collective-permute-start = (f32[6,16,128]{2,1,0:T(8,128)S(1)}, f32[6,16,128]{2,1,0:T(8,128)S(1)}, u32[]{:S(2)}, u32[]{:S(2)}) collective-permute-start(f32[6,16,128]{2,1,0:T(8,128)S(1)} %get-tuple-element.1230), channel_id=1, source_target_pairs={{1,0},{2,1},{3,2},{4,3},{5,4},{6,5},{7,6},{8,7},{9,8},{10,9},{11,1... | collective-permute-start | bytes 147464 | tf_op jit(solution)/shard_map/ppermute | solution.py:45
  20.6 44.9 %collective-permute-start.1 = (f32[6,16,128]{2,1,0:T(8,128)S(1)}, f32[6,16,128]{2,1,0:T(8,128)S(1)}, u32[]{:S(2)}, u32[]{:S(2)}) collective-permute-start(f32[6,16,128]{2,1,0:T(8,128)S(1)} %get-tuple-element.1231), channel_id=1, source_target_pairs={{0,1},{1,2},{2,3},{3,4},{4,5},{5,6},{6,7},{7,8},{8,9},{9,10},{10,1... | collective-permute-start | bytes 147464 | tf_op jit(solution)/shard_map/ppermute | solution.py:44
  21.9 119.7 %copy-start.66 = (f32[256]{0:T(256)}, f32[256]{0:T(256)S(1)}, u32[]{:S(2)}) copy-start(f32[256]{0:T(256)S(1)} %get-tuple-element.1104) | copy-start | bytes 3076
  21.9 130.7 %copy-start.60 = (f32[256]{0:T(256)}, f32[256]{0:T(256)S(1)}, u32[]{:S(2)}) copy-start(f32[256]{0:T(256)S(1)} %get-tuple-element.1105) | copy-start | bytes 3076
  23.3 118.3 %copy-start.47 = (f32[256]{0:T(256)}, f32[256]{0:T(256)S(1)}, u32[]{:S(2)}) copy-start(f32[256]{0:T(256)S(1)} %get-tuple-element.1275) | copy-start | bytes 3076
  30.0 110.2 %copy-start.71 = (f32[256]{0:T(256)}, f32[256]{0:T(256)S(1)}, u32[]{:S(2)}) copy-start(f32[256]{0:T(256)S(1)} %convert_element_type.59) | copy-start | bytes 3076
  50.3 15.9 %copy-start.16 = (bf16[128,128]{1,0:T(8,128)(2,1)S(1)}, bf16[128,128]{1,0:T(8,128)(2,1)}, u32[]{:S(2)}) copy-start(bf16[128,128]{1,0:T(8,128)(2,1)} %param.59) | copy-start | bytes 98308
  50.8 154.0 %copy-start.32 = (f32[16,256]{1,0:T(8,128)}, f32[16,256]{1,0:T(8,128)S(1)}, u32[]{:S(2)}) copy-start(f32[16,256]{1,0:T(8,128)S(1)} %get-tuple-element.1103) | copy-start | bytes 49156
  72.9 36.3 %copy-start.26 = (bf16[1,6,16,256]{3,1,2,0:T(8,128)(2,1)}, bf16[1,6,16,256]{3,1,2,0:T(8,128)(2,1)S(1)}, u32[]{:S(2)}) copy-start(bf16[1,6,16,256]{3,1,2,0:T(8,128)(2,1)S(1)} %copy.23) | copy-start | bytes 147460
  83.8 24.2 %collective-permute-start.2 = (f32[6,16,128]{2,1,0:T(8,128)S(1)}, f32[6,16,128]{2,1,0:T(8,128)S(1)}, u32[]{:S(2)}, u32[]{:S(2)}) collective-permute-start(f32[6,16,128]{2,1,0:T(8,128)S(1)} %get-tuple-element.1214), channel_id=1, source_target_pairs={{1,0},{2,1},{3,2},{4,3},{5,4},{6,5},{7,6},{8,7},{9,8},{10,9},{11,1... | collective-permute-start | bytes 147464 | tf_op jit(solution)/shard_map/ppermute | solution.py:45
  93.8 14.3 %collective-permute-start.3 = (f32[6,16,128]{2,1,0:T(8,128)S(1)}, f32[6,16,128]{2,1,0:T(8,128)S(1)}, u32[]{:S(2)}, u32[]{:S(2)}) collective-permute-start(f32[6,16,128]{2,1,0:T(8,128)S(1)} %get-tuple-element.1215), channel_id=1, source_target_pairs={{0,1},{1,2},{2,3},{3,4},{4,5},{5,6},{6,7},{7,8},{8,9},{9,10},{10,1... | collective-permute-start | bytes 147464 | tf_op jit(solution)/shard_map/ppermute | solution.py:44
  110.6 28.1 %copy-start.11 = (f32[6,16,256]{2,1,0:T(8,128)S(1)}, f32[6,16,256]{2,1,0:T(8,128)}, u32[]{:S(2)}) copy-start(f32[6,16,256]{2,1,0:T(8,128)} %param.57) | copy-start | bytes 294916
  112.0 28.2 %copy-start.107 = (f32[256]{0:T(256)S(1)}, f32[256]{0:T(256)}, u32[]{:S(2)}) copy-start(f32[256]{0:T(256)} %copy-done.105) | copy-start | bytes 3076
  112.0 29.6 %copy-start.94 = (f32[256]{0:T(256)S(1)}, f32[256]{0:T(256)}, u32[]{:S(2)}) copy-start(f32[256]{0:T(256)} %copy-done.92) | copy-start | bytes 3076
  113.3 25.4 %collective-permute-start.4 = (f32[6,16,128]{2,1,0:T(8,128)S(1)}, f32[6,16,128]{2,1,0:T(8,128)S(1)}, u32[]{:S(2)}, u32[]{:S(2)}) collective-permute-start(f32[6,16,128]{2,1,0:T(8,128)S(1)} %get-tuple-element.1193), channel_id=1, source_target_pairs={{1,0},{2,1},{3,2},{4,3},{5,4},{6,5},{7,6},{8,7},{9,8},{10,9},{11,1... | collective-permute-start | bytes 147464 | tf_op jit(solution)/shard_map/ppermute | solution.py:45
  123.2 15.5 %collective-permute-start.5 = (f32[6,16,128]{2,1,0:T(8,128)S(1)}, f32[6,16,128]{2,1,0:T(8,128)S(1)}, u32[]{:S(2)}, u32[]{:S(2)}) collective-permute-start(f32[6,16,128]{2,1,0:T(8,128)S(1)} %get-tuple-element.1194), channel_id=1, source_target_pairs={{0,1},{1,2},{2,3},{3,4},{4,5},{5,6},{6,7},{7,8},{8,9},{9,10},{10,1... | collective-permute-start | bytes 147464 | tf_op jit(solution)/shard_map/ppermute | solution.py:44
  150.4 54.4 %copy-start.72 = (f32[256]{0:T(256)S(1)}, f32[256]{0:T(256)}, u32[]{:S(2)}) copy-start(f32[256]{0:T(256)} %copy-done.71) | copy-start | bytes 3076
  150.7 57.6 %copy-start.48 = (f32[256]{0:T(256)S(1)}, f32[256]{0:T(256)}, u32[]{:S(2)}) copy-start(f32[256]{0:T(256)} %copy-done.47) | copy-start | bytes 3076
  150.9 57.4 %copy-start.95 = (f32[256]{0:T(256)S(1)}, f32[256]{0:T(256)}, u32[]{:S(2)}) copy-start(f32[256]{0:T(256)} %copy-done.92) | copy-start | bytes 3076
  150.9 60.2 %copy-start.75 = (bf16[6,128]{1,0:T(8,128)(2,1)S(1)}, bf16[6,128]{1,0:T(8,128)(2,1)}, u32[]{:S(2)}) copy-start(bf16[6,128]{1,0:T(8,128)(2,1)} %param.60) | copy-start | bytes 4612
  170.9 34.0 %copy-start.59 = (f32[8,256]{1,0:T(8,128)}, f32[8,256]{1,0:T(8,128)S(1)}, u32[]{:S(2)}) copy-start(f32[8,256]{1,0:T(8,128)S(1)} %get-tuple-element.1659) | copy-start | bytes 24580
  170.9 127.5 %reduce-scatter.6.cloned.1.call-start = ((), (), s32[]{:S(2)}) async-start(), calls=%async_computation.4 | async-start | bytes 147456 | tf_op jit(solution)/shard_map/reduce_scatter | solution.py:155
  170.9 21.1 %collective-permute-start.7 = (f32[6,16,128]{2,1,0:T(8,128)S(1)}, f32[6,16,128]{2,1,0:T(8,128)S(1)}, u32[]{:S(2)}, u32[]{:S(2)}) collective-permute-start(f32[6,16,128]{2,1,0:T(8,128)S(1)} %get-tuple-element.1127), channel_id=1, source_target_pairs={{0,31},{1,0},{2,1},{3,2},{4,3},{5,4},{6,5},{7,6},{8,7},{9,8},{10,9... | collective-permute-start | bytes 147464 | tf_op jit(solution)/shard_map/ppermute | solution.py:34
  180.9 11.1 %collective-permute-start.6 = (f32[6,16,128]{2,1,0:T(8,128)S(1)}, f32[6,16,128]{2,1,0:T(8,128)S(1)}, u32[]{:S(2)}, u32[]{:S(2)}) collective-permute-start(f32[6,16,128]{2,1,0:T(8,128)S(1)} %get-tuple-element.1128), channel_id=1, source_target_pairs={{0,1},{1,2},{2,3},{3,4},{4,5},{5,6},{6,7},{7,8},{8,9},{9,10},{10,1... | collective-permute-start | bytes 147464 | tf_op jit(solution)/shard_map/ppermute | solution.py:34
  230.4 30.5 %copy-start.77 = (f32[16,256]{1,0:T(8,128)}, f32[16,256]{1,0:T(8,128)S(1)}, u32[]{:S(2)}) copy-start(f32[16,256]{1,0:T(8,128)S(1)} %pad.471) | copy-start | bytes 49156
  263.5 35.6 %copy-start.33 = (f32[16,256]{1,0:T(8,128)S(1)}, f32[16,256]{1,0:T(8,128)}, u32[]{:S(2)}) copy-start(f32[16,256]{1,0:T(8,128)} %copy-done.32) | copy-start | bytes 49156
  266.8 48.6 %copy-start.96 = (f32[16,256]{1,0:T(8,128)S(1)}, f32[16,256]{1,0:T(8,128)}, u32[]{:S(2)}) copy-start(f32[16,256]{1,0:T(8,128)} %get-tuple-element.1162) | copy-start | bytes 49156
  266.8 48.6 %copy-start.118 = (pred[256]{0:T(512)(128)(4,1)S(1)}, pred[256]{0:T(512)(128)(4,1)}, u32[]{:S(2)}) copy-start(pred[256]{0:T(512)(128)(4,1)} %get-tuple-element.1278) | copy-start | bytes 772
  266.8 48.6 %copy-start.123 = (pred[256]{0:T(512)(128)(4,1)S(1)}, pred[256]{0:T(512)(128)(4,1)}, u32[]{:S(2)}) copy-start(pred[256]{0:T(512)(128)(4,1)} %get-tuple-element.1279) | copy-start | bytes 772
  266.8 49.6 %copy-start.76 = (bf16[6,128]{1,0:T(8,128)(2,1)S(1)}, bf16[6,128]{1,0:T(8,128)(2,1)}, u32[]{:S(2)}) copy-start(bf16[6,128]{1,0:T(8,128)(2,1)} %param.60) | copy-start | bytes 4612
  266.8 211.0 %reduce-scatter.8.cloned.1.call-start = ((), (), s32[]{:S(2)}) async-start(), calls=%async_computation.5 | async-start | bytes 147456 | tf_op jit(solution)/shard_map/reduce_scatter | solution.py:155
  266.9 19.2 %collective-permute-start.9 = (f32[6,16,128]{2,1,0:T(8,128)}, f32[6,16,128]{2,1,0:T(8,128)S(1)}, u32[]{:S(2)}, u32[]{:S(2)}) collective-permute-start(f32[6,16,128]{2,1,0:T(8,128)} %get-tuple-element.1125), channel_id=1, source_target_pairs={{0,31},{1,0},{2,1},{3,2},{4,3},{5,4},{6,5},{7,6},{8,7},{9,8},{10,9... | collective-permute-start | bytes 147464 | tf_op jit(solution)/shard_map/ppermute | solution.py:34
  274.7 11.3 %collective-permute-start.8 = (f32[6,16,128]{2,1,0:T(8,128)}, f32[6,16,128]{2,1,0:T(8,128)S(1)}, u32[]{:S(2)}, u32[]{:S(2)}) collective-permute-start(f32[6,16,128]{2,1,0:T(8,128)} %get-tuple-element.1126), channel_id=1, source_target_pairs={{0,1},{1,2},{2,3},{3,4},{4,5},{5,6},{6,7},{7,8},{8,9},{9,10},{10,1... | collective-permute-start | bytes 147464 | tf_op jit(solution)/shard_map/ppermute | solution.py:34
  334.2 15.3 %copy-start.78 = (f32[16,256]{1,0:T(8,128)}, f32[16,256]{1,0:T(8,128)S(1)}, u32[]{:S(2)}) copy-start(f32[16,256]{1,0:T(8,128)S(1)} %pad.494) | copy-start | bytes 49156
  389.4 277.2 %all-reduce.104.cloned.1.call-start = ((), (), s32[]{:S(2)}) async-start(), calls=%async_computation.6 | async-start | bytes 131072 | tf_op jit(solution)/shard_map/psum | solution.py:237
  394.0 84.6 %copy-start.15 = (f32[6,16,256]{2,1,0:T(8,128)S(1)}, f32[6,16,256]{2,1,0:T(8,128)}, u32[]{:S(2)}) copy-start(f32[6,16,256]{2,1,0:T(8,128)} %copy-done.13) | copy-start | bytes 294916
  394.0 84.6 %copy-start.73 = (f32[256]{0:T(256)S(1)}, f32[256]{0:T(256)}, u32[]{:S(2)}) copy-start(f32[256]{0:T(256)} %copy-done.71) | copy-start | bytes 3076
  394.0 84.6 %copy-start.79 = (f32[16,256]{1,0:T(8,128)S(1)}, f32[16,256]{1,0:T(8,128)}, u32[]{:S(2)}) copy-start(f32[16,256]{1,0:T(8,128)} %copy-done.78) | copy-start | bytes 49156
  394.0 84.6 %copy-start.80 = (f32[16,256]{1,0:T(8,128)S(1)}, f32[16,256]{1,0:T(8,128)}, u32[]{:S(2)}) copy-start(f32[16,256]{1,0:T(8,128)} %pad.495) | copy-start | bytes 49156
  394.0 84.6 %copy-start.110 = (f32[256]{0:T(256)S(1)}, f32[256]{0:T(256)}, u32[]{:S(2)}) copy-start(f32[256]{0:T(256)} %get-tuple-element.904) | copy-start | bytes 3076
  394.0 84.6 %copy-start.12 = (f32[6,16,256]{2,1,0:T(8,128)S(1)}, f32[6,16,256]{2,1,0:T(8,128)}, u32[]{:S(2)}) copy-start(f32[6,16,256]{2,1,0:T(8,128)} %param.57) | copy-start | bytes 294916
  394.1 83.7 %collective-permute-start.10 = (f32[6,16,128]{2,1,0:T(8,128)S(1)}, f32[6,16,128]{2,1,0:T(8,128)S(1)}, u32[]{:S(2)}, u32[]{:S(2)}) collective-permute-start(f32[6,16,128]{2,1,0:T(8,128)S(1)} %copy-done.104), channel_id=1, source_target_pairs={{0,1},{1,2},{2,3},{3,4},{4,5},{5,6},{6,7},{7,8},{8,9},{9,10},{10,1... | collective-permute-start | bytes 147464 | tf_op jit(solution)/shard_map/ppermute | solution.py:34
  395.7 82.1 %collective-permute-start.11 = (f32[6,16,128]{2,1,0:T(8,128)S(1)}, f32[6,16,128]{2,1,0:T(8,128)S(1)}, u32[]{:S(2)}, u32[]{:S(2)}) collective-permute-start(f32[6,16,128]{2,1,0:T(8,128)S(1)} %copy-done.103), channel_id=1, source_target_pairs={{0,31},{1,0},{2,1},{3,2},{4,3},{5,4},{6,5},{7,6},{8,7},{9,8},{10,9... | collective-permute-start | bytes 147464 | tf_op jit(solution)/shard_map/ppermute | solution.py:34
  (106 other events, 383.8 us)
Sparse Core Ops, SparseCore 0:
  171.0 33.0 reduce-scatter.3
  267.0 31.3 reduce-scatter.5
  389.5 30.6 reduce-scatter.7
  427.1 239.4 all-reduce.103
where the time goes:
time: 680 us; the launch traced here: 675 us
  waiting for transfers between devices  232 us (34%)
  blocking collectives  190 us (28%)
  other arithmetic  85.1 us (13%)
  local copies, waits for them, and re-layouts  63.4 us (9%)
  starting transfers between devices  60.1 us (9%)
  matrix products  26.9 us (4%)
  between operations  16.2 us (2%)
    psum x1, waiting for transfers between devices, on_device(): lax.psum((TIME_STEP * (grads_two[0] + grads_one[0] + grads_zero[0]), TIME...  187 us
    psum x1, blocking collectives, on_device(): lax.psum((TIME_STEP * (grads_two[0] + grads_one[0] + grads_zero[0]), TIME...  73.1 us
    all_gather x7, blocking collectives, prefix(): everything = jax.tree.map(lambda part: lax.all_gather(part, axis), shard)  73 us
    all_gather x3, blocking collectives, heating(): lax.all_gather(theta, 'gz', axis=0, tiled=True)  43.7 us
    select_n x48, other arithmetic, step(): return jax.tree.map(lambda a, b: jnp.where(reached, a, b), new, before)  35.2 us
    ppermute x3, starting transfers between devices, padded_2(): after = lax.ppermute(first, axis, down)  32.3 us
    ppermute x6, starting transfers between devices, passed_along(): lax.ppermute(shard, axis, [(i, (i + by) % length) for i in range(length)])  27.5 us
    reduce_scatter x3, waiting for transfers between devices, heating_adjoint(): lax.psum_scatter(lax.dot_general(own_rows, lead_theta, (((0,), (0,)), (()...  24.4 us
  transfers between devices with their start and end apart: 16, of which 5 were waited for; matrix products, arithmetic and copies ran while one was open for 3% of the time, Pallas kernels for 0%

commit v1 on v0

--- a/solution.py
+++ b/solution.py
@@ -235,12 +235,15 @@
     back_zero, grads_zero = section_adjoint(padded_zero, cot_one)
     grad_state = grad_state + cot_one + TIME_STEP * back_zero
     totals = lax.psum(
-        (
-            TIME_STEP * (grads_two[0] + grads_one[0] + grads_zero[0]),
-            TIME_STEP * (grads_two[1] + grads_one[1] + grads_zero[1]),
-            TIME_STEP * (grads_two[2] + grads_one[2] + grads_zero[2]),
+        lax.psum(
+            (
+                TIME_STEP * (grads_two[0] + grads_one[0] + grads_zero[0]),
+                TIME_STEP * (grads_two[1] + grads_one[1] + grads_zero[1]),
+                TIME_STEP * (grads_two[2] + grads_one[2] + grads_zero[2]),
+            ),
+            "gz",
         ),
-        ("gz", "gx"),
+        "gx",
     )
     return (new_state, grad_state, totals[0], totals[1], totals[2])
 

time: 680 us -> 999 us (1.47)
  waiting for transfers between devices: 232 us -> 440 us
  blocking collectives: 190 us -> 336 us
  other arithmetic: 85.1 us -> 56 us
    psum x0 -> x1, waiting for transfers between devices: none -> 395 us  [on_device(): lax.psum(lax.psum((TIME_STEP * (grads_two[0] + grads_one[0] + grads_zero[...]
    psum x0 -> x1, blocking collectives: none -> 197 us  [on_device(): lax.psum(lax.psum((TIME_STEP * (grads_two[0] + grads_one[0] + grads_zero[...]
    psum x1, waiting for transfers between devices: 187 us -> 0.02 us  [on_device(): lax.psum((TIME_STEP * (grads_two[0] + grads_one[0] + grads_zero[0]), TIME...]
    psum x1, blocking collectives: 73.1 us -> 22.8 us  [on_device(): lax.psum((TIME_STEP * (grads_two[0] + grads_one[0] + grads_zero[0]), TIME...]
    select_n x48, other arithmetic: 35.2 us -> 18.6 us  [step(): return jax.tree.map(lambda a, b: jnp.where(reached, a, b), new, before)]
  transfers between devices with their start and end apart: 16 -> 17, of which waited for: 5 -> 5; matrix products, arithmetic and copies ran while one was open for 3% -> 2% of each run, Pallas kernels for 0% -> 0%
where the time goes in v1:
time: 999 us; the launch traced here: 986 us
  waiting for transfers between devices  440 us (44%)
  blocking collectives  336 us (34%)
  starting transfers between devices  57.2 us (6%)
  other arithmetic  56 us (6%)
  local copies, waits for them, and re-layouts  53.6 us (5%)
  matrix products  25.1 us (3%)
  between operations  16.3 us (2%)
    psum x1, waiting for transfers between devices, on_device(): lax.psum(lax.psum((TIME_STEP * (grads_two[0] + grads_one[0] + grads_zero[...  395 us
    psum x1, blocking collectives, on_device(): lax.psum(lax.psum((TIME_STEP * (grads_two[0] + grads_one[0] + grads_zero[...  197 us
    all_gather x7, blocking collectives, prefix(): everything = jax.tree.map(lambda part: lax.all_gather(part, axis), shard)  73 us
    all_gather x3, blocking collectives, heating(): lax.all_gather(theta, 'gz', axis=0, tiled=True)  43.7 us
    ppermute x3, starting transfers between devices, padded_2(): after = lax.ppermute(first, axis, down)  32.3 us
    ppermute x6, starting transfers between devices, passed_along(): lax.ppermute(shard, axis, [(i, (i + by) % length) for i in range(length)])  24.8 us
    reduce_scatter x3, waiting for transfers between devices, heating_adjoint(): lax.psum_scatter(lax.dot_general(own_rows, lead_theta, (((0,), (0,)), (()...  24.4 us
    psum x1, blocking collectives, on_device(): lax.psum((TIME_STEP * (grads_two[0] + grads_one[0] + grads_zero[0]), TIME...  22.8 us
  transfers between devices with their start and end apart: 17, of which 5 were waited for; matrix products, arithmetic and copies ran while one was open for 2% of the time, Pallas kernels for 0%

profile of v1, /device:TPU:1, one launch (start us, length us, event | category | flops | bytes accessed | tf_op | source)
XLA Modules:
  0.0 986.0 jit_solution(12080212071347931494)
XLA Ops:
  8.1 12.5 %collective-permute-start = (f32[6,16,128]{2,1,0:T(8,128)S(1)}, f32[6,16,128]{2,1,0:T(8,128)S(1)}, u32[]{:S(2)}, u32[]{:S(2)}) collective-permute-start(f32[6,16,128]{2,1,0:T(8,128)S(1)} %get-tuple-element.1232), channel_id=1, source_target_pairs={{1,0},{2,1},{3,2},{4,3},{5,4},{6,5},{7,6},{8,7},{9,8},{10,9},{11,1... | collective-permute-start | bytes 147464 | tf_op jit(solution)/shard_map/ppermute | solution.py:45
  21.9 1.4 bitcast_multiply_fusion
  23.7 1.5 fusion.147
  25.2 1.5 fusion.146
  27.8 1.6 fusion.145
  30.5 11.1 %all-gather.3 = f32[8,1,256]{2,1,0:T(1,128)S(1)} all-gather(f32[1,1,256]{2,1,0:T(1,128)S(1)} %add_bitcast_fusion.6), channel_id=1, replica_groups=mesh['gz'=8,'gx'=32] {'gz'}, dimensions={0}, use_global_device_ids=true | all-gather | bytes 9216 | tf_op jit(solution)/shard_map/all_gather | solution.py:16
  41.6 8.7 all-gather.4
  51.5 14.0 %all-gather = f32[1,128,256]{2,1,0:T(8,128)S(1)} all-gather(f32[1,16,256]{2,1,0:T(8,128)S(1)} %slice-done), channel_id=2, replica_groups=mesh['gz'=8,'gx'=32] {'gz'}, dimensions={1}, use_global_device_ids=true | all-gather | bytes 147456 | tf_op jit(solution)/shard_map/all_gather | solution.py:146
  73.2 10.1 %all-gather.5 = f32[8,1,256]{2,1,0:T(1,128)S(1)} all-gather(f32[1,1,256]{2,1,0:T(1,128)S(1)} %add_bitcast_fusion.4), channel_id=1, replica_groups=mesh['gz'=8,'gx'=32] {'gz'}, dimensions={0}, use_global_device_ids=true | all-gather | bytes 9216 | tf_op jit(solution)/shard_map/all_gather | solution.py:16
  84.4 9.9 collective-permute-start.2
  94.3 14.3 %all-gather.1 = f32[1,128,256]{2,1,0:T(8,128)S(1)} all-gather(f32[1,16,256]{2,1,0:T(8,128)S(1)} %get-tuple-element.1174), channel_id=3, replica_groups=mesh['gz'=8,'gx'=32] {'gz'}, dimensions={1}, use_global_device_ids=true | all-gather | bytes 147456 | tf_op jit(solution)/shard_map/all_gather | solution.py:146
  113.2 9.9 %collective-permute-start.4 = (f32[6,16,128]{2,1,0:T(8,128)S(1)}, f32[6,16,128]{2,1,0:T(8,128)S(1)}, u32[]{:S(2)}, u32[]{:S(2)}) collective-permute-start(f32[6,16,128]{2,1,0:T(8,128)S(1)} %get-tuple-element.1195), channel_id=1, source_target_pairs={{1,0},{2,1},{3,2},{4,3},{5,4},{6,5},{7,6},{8,7},{9,8},{10,9},{11,1... | collective-permute-start | bytes 147464 | tf_op jit(solution)/shard_map/ppermute | solution.py:45
  123.2 15.5 %all-gather.2 = f32[1,128,256]{2,1,0:T(8,128)} all-gather(f32[1,16,256]{2,1,0:T(8,128)S(1)} %get-tuple-element.1190), channel_id=4, replica_groups=mesh['gz'=8,'gx'=32] {'gz'}, dimensions={1}, use_global_device_ids=true | all-gather | bytes 147456 | tf_op jit(solution)/shard_map/all_gather | solution.py:146
  138.7 1.5 broadcast_multiply_fusion
  153.4 8.7 all-gather.7
  162.2 9.5 while.111
  162.8 1.3 add_select_fusion.15
  164.1 1.3 add_select_fusion.15
  165.3 1.3 add_select_fusion.15
  166.6 1.3 add_select_fusion.15
  167.9 1.3 add_select_fusion.15
  171.7 9.9 %collective-permute-start.7 = (f32[6,16,128]{2,1,0:T(8,128)S(1)}, f32[6,16,128]{2,1,0:T(8,128)S(1)}, u32[]{:S(2)}, u32[]{:S(2)}) collective-permute-start(f32[6,16,128]{2,1,0:T(8,128)S(1)} %get-tuple-element.1129), channel_id=1, source_target_pairs={{0,31},{1,0},{2,1},{3,2},{4,3},{5,4},{6,5},{7,6},{8,7},{9,8},{10,9... | collective-permute-start | bytes 147464 | tf_op jit(solution)/shard_map/ppermute | solution.py:34
  181.7 11.1 %collective-permute-done.6 = f32[6,16,128]{2,1,0:T(8,128)S(1)} collective-permute-done((f32[6,16,128]{2,1,0:T(8,128)S(1)}, f32[6,16,128]{2,1,0:T(8,128)S(1)}, u32[]{:S(2)}, u32[]{:S(2)}) %collective-permute-start.6) | collective-permute-done | bytes 49184 | tf_op jit(solution)/shard_map/ppermute | solution.py:34
  192.8 12.0 %reduce-scatter.4.cloned.1.call-done = f32[16,256]{1,0:T(8,128)} async-done(((f32[128,256]{1,0:T(8,128)}), f32[16,256]{1,0:T(8,128)}) %reduce-scatter.4.cloned.1.call-update) | async-done | bytes 16400 | tf_op jit(solution)/shard_map/reduce_scatter | solution.py:155
  211.8 2.2 fusion.2
  219.0 1.9 pad.467
  220.9 1.9 pad.468
  222.8 1.3 add.1088
  226.0 1.9 pad.470
  227.9 1.3 add.1090
  231.2 1.9 pad.472
  233.9 12.0 %all-gather.8 = f32[8,1,256]{2,1,0:T(1,128)S(1)} all-gather(f32[1,1,256]{2,1,0:T(1,128)S(1)} %add_bitcast_fusion.1), channel_id=1, replica_groups=mesh['gz'=8,'gx'=32] {'gz'}, dimensions={0}, use_global_device_ids=true | all-gather | bytes 9216 | tf_op jit(solution)/shard_map/all_gather | solution.py:16
  246.5 14.5 %while.112 = (s32[]{:T(128)}, f32[256]{0:T(256)}, s32[]{:T(128)}, f32[8,256]{1,0:T(8,128)}, f32[8,256]{1,0:T(8,128)}, /*index=5*/s32[]{:T(128)}, s32[]{:T(128)}) while((s32[]{:T(128)}, f32[256]{0:T(256)}, s32[]{:T(128)}, f32[8,256]{1,0:T(8,128)}, f32[8,256]{1,0:T(8,128)}, /*index=5*/s32[]{:T(128)}, s32[]{:T(128)}) %tuple.461), condition=%wide.region_15.16_spmd.clone, body=%wide.region_14.15_spmd.clone.sunk | while | flops 1028 | bytes 8301 | solution.py:29
  261.0 2.6 convolution_add_fusion.5
  263.6 2.4 convolution_add_fusion.1
  267.0 7.8 collective-permute-start.9
  275.8 10.3 %collective-permute-done.8 = f32[6,16,128]{2,1,0:T(8,128)S(1)} collective-permute-done((f32[6,16,128]{2,1,0:T(8,128)}, f32[6,16,128]{2,1,0:T(8,128)S(1)}, u32[]{:S(2)}, u32[]{:S(2)}) %collective-permute-start.8) | collective-permute-done | bytes 49184 | tf_op jit(solution)/shard_map/ppermute | solution.py:34
  286.2 12.4 %reduce-scatter.6.cloned.1.call-done = f32[16,256]{1,0:T(8,128)} async-done(((f32[128,256]{1,0:T(8,128)}), f32[16,256]{1,0:T(8,128)}) %reduce-scatter.6.cloned.1.call-update) | async-done | bytes 16400 | tf_op jit(solution)/shard_map/reduce_scatter | solution.py:155
  300.0 1.7 multiply_reduce_fusion.1
  312.3 12.0 %all-gather.9 = f32[8,1,256]{2,1,0:T(1,128)S(1)} all-gather(f32[1,1,256]{2,1,0:T(1,128)S(1)} %add_bitcast_fusion), channel_id=1, replica_groups=mesh['gz'=8,'gx'=32] {'gz'}, dimensions={0}, use_global_device_ids=true | all-gather | bytes 9216 | tf_op jit(solution)/shard_map/all_gather | solution.py:16
  324.4 5.9 while.113
  330.3 10.4 %all-gather.6 = f32[8,1,256]{2,1,0:T(1,128)S(1)} all-gather(f32[1,1,256]{2,1,0:T(1,128)S(1)} %add_bitcast_fusion.3), channel_id=1, replica_groups=mesh['gz'=8,'gx'=32] {'gz'}, dimensions={0}, use_global_device_ids=true | all-gather | bytes 9216 | tf_op jit(solution)/shard_map/all_gather | solution.py:16
  340.7 5.9 while.110
  353.7 7.0 collective-permute-start.11
  361.4 22.8 %all-reduce.102 = (f32[128,12]{0,1:T(8,128)S(1)}, f32[6,128]{1,0:T(8,128)S(1)}) all-reduce(f32[128,12]{0,1:T(8,128)S(1)} %copy-done.108, f32[6,128]{1,0:T(8,128)S(1)} %copy-done.120), channel_id=1, replica_groups=mesh['gz'=8,'gx'=32] {'gz'}, use_global_device_ids=true, to_apply=%region_21.22 | all-reduce | flops 2304 | bytes 18432 | tf_op jit(solution)/shard_map/psum | solution.py:238
  384.2 196.8 %all-reduce.101 = (f32[128,12]{0,1:T(8,128)}, f32[6,128]{1,0:T(8,128)}) all-reduce(f32[128,12]{0,1:T(8,128)S(1)} %get-tuple-element.1081, f32[6,128]{1,0:T(8,128)S(1)} %get-tuple-element.1082), channel_id=1, replica_groups=mesh['gz'=8,'gx'=32] {'gx'}, use_global_device_ids=true, to_apply=%region_22.23 | all-reduce | flops 2304 | bytes 18432 | tf_op jit(solution)/shard_map/psum | solution.py:237
  583.3 394.6 %all-reduce.108.cloned.1.call-done = f32[128,128]{1,0:T(8,128)} async-done(((f32[128,128]{1,0:T(8,128)}), f32[128,128]{1,0:T(8,128)}) %all-reduce.108.cloned.1.call-update) | async-done | bytes 65552 | tf_op jit(solution)/shard_map/psum | solution.py:237
  978.0 1.5 copy.128
  (713 shorter events, 101.7 us)
Async XLA Ops:
  7.2 62.3 %copy-start = (f32[128,128]{1,0:T(8,128)S(1)}, f32[128,128]{1,0:T(8,128)}, u32[]{:S(2)}) copy-start(f32[128,128]{1,0:T(8,128)} %param.61) | copy-start | bytes 196612
  7.2 44.3 %slice-start = ((f32[6,16,256]{2,1,0:T(8,128)}), f32[1,16,256]{2,1,0:T(8,128)S(1)}, s32[]{:S(2)}) async-start(f32[6,16,256]{2,1,0:T(8,128)} %param.56), calls=%async_computation.8 | async-start | bytes 32768 | tf_op jit(solution)/shard_map/slice | solution.py:180
  7.2 58.3 %copy-start.7 = (f32[6,16,256]{2,1,0:T(8,128)S(1)}, f32[6,16,256]{2,1,0:T(8,128)}, u32[]{:S(2)}) copy-start(f32[6,16,256]{2,1,0:T(8,128)} %param.56) | copy-start | bytes 294916
  7.2 58.5 %copy-start.57 = (bf16[128,12]{0,1:T(8,128)(2,1)S(1)}, bf16[128,12]{0,1:T(8,128)(2,1)}, u32[]{:S(2)}) copy-start(bf16[128,12]{0,1:T(8,128)(2,1)} %param.58) | copy-start | bytes 9220
  7.2 197.6 %reduce-scatter.4.cloned.1.call-start = ((), (), s32[]{:S(2)}) async-start(), calls=%async_computation.3 | async-start | bytes 147456 | tf_op jit(solution)/shard_map/reduce_scatter | solution.py:155
  8.1 57.4 %collective-permute-start = (f32[6,16,128]{2,1,0:T(8,128)S(1)}, f32[6,16,128]{2,1,0:T(8,128)S(1)}, u32[]{:S(2)}, u32[]{:S(2)}) collective-permute-start(f32[6,16,128]{2,1,0:T(8,128)S(1)} %get-tuple-element.1232), channel_id=1, source_target_pairs={{1,0},{2,1},{3,2},{4,3},{5,4},{6,5},{7,6},{8,7},{9,8},{10,9},{11,1... | collective-permute-start | bytes 147464 | tf_op jit(solution)/shard_map/ppermute | solution.py:45
  20.6 44.9 %collective-permute-start.1 = (f32[6,16,128]{2,1,0:T(8,128)S(1)}, f32[6,16,128]{2,1,0:T(8,128)S(1)}, u32[]{:S(2)}, u32[]{:S(2)}) collective-permute-start(f32[6,16,128]{2,1,0:T(8,128)S(1)} %get-tuple-element.1233), channel_id=1, source_target_pairs={{0,1},{1,2},{2,3},{3,4},{4,5},{5,6},{6,7},{7,8},{8,9},{9,10},{10,1... | collective-permute-start | bytes 147464 | tf_op jit(solution)/shard_map/ppermute | solution.py:44
  21.9 119.6 %copy-start.60 = (f32[256]{0:T(256)}, f32[256]{0:T(256)S(1)}, u32[]{:S(2)}) copy-start(f32[256]{0:T(256)S(1)} %get-tuple-element.1106) | copy-start | bytes 3076
  21.9 130.8 %copy-start.54 = (f32[256]{0:T(256)}, f32[256]{0:T(256)S(1)}, u32[]{:S(2)}) copy-start(f32[256]{0:T(256)S(1)} %get-tuple-element.1107) | copy-start | bytes 3076
  23.4 118.3 %copy-start.41 = (f32[256]{0:T(256)}, f32[256]{0:T(256)S(1)}, u32[]{:S(2)}) copy-start(f32[256]{0:T(256)S(1)} %get-tuple-element.1277) | copy-start | bytes 3076
  30.1 110.1 %copy-start.65 = (f32[256]{0:T(256)}, f32[256]{0:T(256)S(1)}, u32[]{:S(2)}) copy-start(f32[256]{0:T(256)S(1)} %convert_element_type.59) | copy-start | bytes 3076
  50.8 154.7 %copy-start.26 = (f32[16,256]{1,0:T(8,128)}, f32[16,256]{1,0:T(8,128)S(1)}, u32[]{:S(2)}) copy-start(f32[16,256]{1,0:T(8,128)S(1)} %get-tuple-element.1105) | copy-start | bytes 49156
  73.0 36.8 %copy-start.21 = (bf16[1,6,16,256]{3,1,2,0:T(8,128)(2,1)}, bf16[1,6,16,256]{3,1,2,0:T(8,128)(2,1)S(1)}, u32[]{:S(2)}) copy-start(bf16[1,6,16,256]{3,1,2,0:T(8,128)(2,1)S(1)} %copy.23) | copy-start | bytes 147460
  84.4 24.1 %collective-permute-start.2 = (f32[6,16,128]{2,1,0:T(8,128)S(1)}, f32[6,16,128]{2,1,0:T(8,128)S(1)}, u32[]{:S(2)}, u32[]{:S(2)}) collective-permute-start(f32[6,16,128]{2,1,0:T(8,128)S(1)} %get-tuple-element.1216), channel_id=1, source_target_pairs={{1,0},{2,1},{3,2},{4,3},{5,4},{6,5},{7,6},{8,7},{9,8},{10,9},{11,1... | collective-permute-start | bytes 147464 | tf_op jit(solution)/shard_map/ppermute | solution.py:45
  94.3 14.3 %collective-permute-start.3 = (f32[6,16,128]{2,1,0:T(8,128)S(1)}, f32[6,16,128]{2,1,0:T(8,128)S(1)}, u32[]{:S(2)}, u32[]{:S(2)}) collective-permute-start(f32[6,16,128]{2,1,0:T(8,128)S(1)} %get-tuple-element.1217), channel_id=1, source_target_pairs={{0,1},{1,2},{2,3},{3,4},{4,5},{5,6},{6,7},{7,8},{8,9},{9,10},{10,1... | collective-permute-start | bytes 147464 | tf_op jit(solution)/shard_map/ppermute | solution.py:44
  113.2 25.4 %collective-permute-start.4 = (f32[6,16,128]{2,1,0:T(8,128)S(1)}, f32[6,16,128]{2,1,0:T(8,128)S(1)}, u32[]{:S(2)}, u32[]{:S(2)}) collective-permute-start(f32[6,16,128]{2,1,0:T(8,128)S(1)} %get-tuple-element.1195), channel_id=1, source_target_pairs={{1,0},{2,1},{3,2},{4,3},{5,4},{6,5},{7,6},{8,7},{9,8},{10,9},{11,1... | collective-permute-start | bytes 147464 | tf_op jit(solution)/shard_map/ppermute | solution.py:45
  123.2 15.5 %collective-permute-start.5 = (f32[6,16,128]{2,1,0:T(8,128)S(1)}, f32[6,16,128]{2,1,0:T(8,128)S(1)}, u32[]{:S(2)}, u32[]{:S(2)}) collective-permute-start(f32[6,16,128]{2,1,0:T(8,128)S(1)} %get-tuple-element.1196), channel_id=1, source_target_pairs={{0,1},{1,2},{2,3},{3,4},{4,5},{5,6},{6,7},{7,8},{8,9},{9,10},{10,1... | collective-permute-start | bytes 147464 | tf_op jit(solution)/shard_map/ppermute | solution.py:44
  150.5 55.1 %copy-start.66 = (f32[256]{0:T(256)S(1)}, f32[256]{0:T(256)}, u32[]{:S(2)}) copy-start(f32[256]{0:T(256)} %copy-done.65) | copy-start | bytes 3076
  150.7 58.2 %copy-start.42 = (f32[256]{0:T(256)S(1)}, f32[256]{0:T(256)}, u32[]{:S(2)}) copy-start(f32[256]{0:T(256)} %copy-done.41) | copy-start | bytes 3076
  150.9 58.1 %copy-start.89 = (f32[256]{0:T(256)S(1)}, f32[256]{0:T(256)}, u32[]{:S(2)}) copy-start(f32[256]{0:T(256)} %copy-done.86) | copy-start | bytes 3076
  150.9 60.9 %copy-start.69 = (bf16[6,128]{1,0:T(8,128)(2,1)S(1)}, bf16[6,128]{1,0:T(8,128)(2,1)}, u32[]{:S(2)}) copy-start(bf16[6,128]{1,0:T(8,128)(2,1)} %param.60) | copy-start | bytes 4612
  171.7 126.9 %reduce-scatter.6.cloned.1.call-start = ((), (), s32[]{:S(2)}) async-start(), calls=%async_computation.4 | async-start | bytes 147456 | tf_op jit(solution)/shard_map/reduce_scatter | solution.py:155
  171.7 21.1 %collective-permute-start.7 = (f32[6,16,128]{2,1,0:T(8,128)S(1)}, f32[6,16,128]{2,1,0:T(8,128)S(1)}, u32[]{:S(2)}, u32[]{:S(2)}) collective-permute-start(f32[6,16,128]{2,1,0:T(8,128)S(1)} %get-tuple-element.1129), channel_id=1, source_target_pairs={{0,31},{1,0},{2,1},{3,2},{4,3},{5,4},{6,5},{7,6},{8,7},{9,8},{10,9... | collective-permute-start | bytes 147464 | tf_op jit(solution)/shard_map/ppermute | solution.py:34
  181.7 11.1 %collective-permute-start.6 = (f32[6,16,128]{2,1,0:T(8,128)S(1)}, f32[6,16,128]{2,1,0:T(8,128)S(1)}, u32[]{:S(2)}, u32[]{:S(2)}) collective-permute-start(f32[6,16,128]{2,1,0:T(8,128)S(1)} %get-tuple-element.1130), channel_id=1, source_target_pairs={{0,1},{1,2},{2,3},{3,4},{4,5},{5,6},{6,7},{7,8},{8,9},{9,10},{10,1... | collective-permute-start | bytes 147464 | tf_op jit(solution)/shard_map/ppermute | solution.py:34
  263.6 35.6 %copy-start.27 = (f32[16,256]{1,0:T(8,128)S(1)}, f32[16,256]{1,0:T(8,128)}, u32[]{:S(2)}) copy-start(f32[16,256]{1,0:T(8,128)} %copy-done.26) | copy-start | bytes 49156
  266.9 42.2 %copy-start.91 = (f32[16,256]{1,0:T(8,128)S(1)}, f32[16,256]{1,0:T(8,128)}, u32[]{:S(2)}) copy-start(f32[16,256]{1,0:T(8,128)} %get-tuple-element.1164) | copy-start | bytes 49156
  266.9 42.2 %copy-start.113 = (pred[256]{0:T(512)(128)(4,1)S(1)}, pred[256]{0:T(512)(128)(4,1)}, u32[]{:S(2)}) copy-start(pred[256]{0:T(512)(128)(4,1)} %get-tuple-element.1280) | copy-start | bytes 772
  266.9 42.2 %copy-start.118 = (pred[256]{0:T(512)(128)(4,1)S(1)}, pred[256]{0:T(512)(128)(4,1)}, u32[]{:S(2)}) copy-start(pred[256]{0:T(512)(128)(4,1)} %get-tuple-element.1281) | copy-start | bytes 772
  266.9 45.2 %copy-start.62 = (f32[256]{0:T(256)S(1)}, f32[256]{0:T(256)}, u32[]{:S(2)}) copy-start(f32[256]{0:T(256)} %copy-done.60) | copy-start | bytes 3076
  266.9 45.3 %copy-start.56 = (f32[256]{0:T(256)S(1)}, f32[256]{0:T(256)}, u32[]{:S(2)}) copy-start(f32[256]{0:T(256)} %copy-done.54) | copy-start | bytes 3076
  266.9 57.5 %copy-start.103 = (f32[256]{0:T(256)S(1)}, f32[256]{0:T(256)}, u32[]{:S(2)}) copy-start(f32[256]{0:T(256)} %custom-call.5) | copy-start | bytes 3076
  266.9 73.8 %copy-start.101 = (f32[256]{0:T(256)S(1)}, f32[256]{0:T(256)}, u32[]{:S(2)}) copy-start(f32[256]{0:T(256)} %custom-call.2) | copy-start | bytes 3076
  266.9 314.2 %all-reduce.106.cloned.1.call-start = ((), (), s32[]{:S(2)}) async-start(), calls=%async_computation.6 | async-start | bytes 131072 | tf_op jit(solution)/shard_map/psum | solution.py:238
  267.0 19.2 %collective-permute-start.9 = (f32[6,16,128]{2,1,0:T(8,128)}, f32[6,16,128]{2,1,0:T(8,128)S(1)}, u32[]{:S(2)}, u32[]{:S(2)}) collective-permute-start(f32[6,16,128]{2,1,0:T(8,128)} %get-tuple-element.1127), channel_id=1, source_target_pairs={{0,31},{1,0},{2,1},{3,2},{4,3},{5,4},{6,5},{7,6},{8,7},{9,8},{10,9... | collective-permute-start | bytes 147464 | tf_op jit(solution)/shard_map/ppermute | solution.py:34
  274.8 11.3 %collective-permute-start.8 = (f32[6,16,128]{2,1,0:T(8,128)}, f32[6,16,128]{2,1,0:T(8,128)S(1)}, u32[]{:S(2)}, u32[]{:S(2)}) collective-permute-start(f32[6,16,128]{2,1,0:T(8,128)} %get-tuple-element.1128), channel_id=1, source_target_pairs={{0,1},{1,2},{2,3},{3,4},{4,5},{5,6},{6,7},{7,8},{8,9},{9,10},{10,1... | collective-permute-start | bytes 147464 | tf_op jit(solution)/shard_map/ppermute | solution.py:34
  275.8 71.5 %copy-start.70 = (bf16[6,128]{1,0:T(8,128)(2,1)S(1)}, bf16[6,128]{1,0:T(8,128)(2,1)}, u32[]{:S(2)}) copy-start(bf16[6,128]{1,0:T(8,128)(2,1)} %param.60) | copy-start | bytes 4612
  312.2 35.7 %copy-start.119 = (f32[6,128]{1,0:T(8,128)S(1)}, f32[6,128]{1,0:T(8,128)}, u32[]{:S(2)}) copy-start(f32[6,128]{1,0:T(8,128)} %convolution_add_fusion.5) | copy-start | bytes 9220
  312.3 35.0 %copy-start.74 = (f32[16,256]{1,0:T(8,128)}, f32[16,256]{1,0:T(8,128)S(1)}, u32[]{:S(2)}) copy-start(f32[16,256]{1,0:T(8,128)S(1)} %pad.495) | copy-start | bytes 49156
  352.3 228.9 %reduce-scatter.8.cloned.1.call-start = ((), (), s32[]{:S(2)}) async-start(), calls=%async_computation.5 | async-start | bytes 147456 | tf_op jit(solution)/shard_map/reduce_scatter | solution.py:155
  352.5 229.4 %copy-start.67 = (f32[256]{0:T(256)S(1)}, f32[256]{0:T(256)}, u32[]{:S(2)}) copy-start(f32[256]{0:T(256)} %copy-done.65) | copy-start | bytes 3076
  352.5 229.4 %copy-start.73 = (f32[16,256]{1,0:T(8,128)S(1)}, f32[16,256]{1,0:T(8,128)}, u32[]{:S(2)}) copy-start(f32[16,256]{1,0:T(8,128)} %copy-done.72) | copy-start | bytes 49156
  352.5 229.4 %copy-start.75 = (f32[16,256]{1,0:T(8,128)S(1)}, f32[16,256]{1,0:T(8,128)}, u32[]{:S(2)}) copy-start(f32[16,256]{1,0:T(8,128)} %copy-done.74) | copy-start | bytes 49156
  352.6 229.4 %copy-start.94 = (f32[16,256]{1,0:T(8,128)S(1)}, f32[16,256]{1,0:T(8,128)}, u32[]{:S(2)}) copy-start(f32[16,256]{1,0:T(8,128)} %rev.15) | copy-start | bytes 49156
  352.6 229.4 %copy-start.105 = (f32[256]{0:T(256)S(1)}, f32[256]{0:T(256)}, u32[]{:S(2)}) copy-start(f32[256]{0:T(256)} %copy-done.104) | copy-start | bytes 3076
  352.6 229.4 %copy-start.10 = (f32[6,16,256]{2,1,0:T(8,128)S(1)}, f32[6,16,256]{2,1,0:T(8,128)}, u32[]{:S(2)}) copy-start(f32[6,16,256]{2,1,0:T(8,128)} %param.57) | copy-start | bytes 294916
  353.7 227.4 %collective-permute-start.11 = (f32[6,16,128]{2,1,0:T(8,128)S(1)}, f32[6,16,128]{2,1,0:T(8,128)S(1)}, u32[]{:S(2)}, u32[]{:S(2)}) collective-permute-start(f32[6,16,128]{2,1,0:T(8,128)S(1)} %get-tuple-element.1125), channel_id=1, source_target_pairs={{0,31},{1,0},{2,1},{3,2},{4,3},{5,4},{6,5},{7,6},{8,7},{9,8},{10,9... | collective-permute-start | bytes 147464 | tf_op jit(solution)/shard_map/ppermute | solution.py:34
  360.7 220.4 %collective-permute-start.10 = (f32[6,16,128]{2,1,0:T(8,128)S(1)}, f32[6,16,128]{2,1,0:T(8,128)S(1)}, u32[]{:S(2)}, u32[]{:S(2)}) collective-permute-start(f32[6,16,128]{2,1,0:T(8,128)S(1)} %get-tuple-element.1126), channel_id=1, source_target_pairs={{0,1},{1,2},{2,3},{3,4},{4,5},{5,6},{6,7},{7,8},{8,9},{9,10},{10,1... | collective-permute-start | bytes 147464 | tf_op jit(solution)/shard_map/ppermute | solution.py:34
  361.3 616.7 %all-reduce.108.cloned.1.call-start = ((), (), s32[]{:S(2)}) async-start(), calls=%async_computation.7 | async-start | bytes 131072 | tf_op jit(solution)/shard_map/psum | solution.py:237
  (99 other events, 489.4 us)
Sparse Core Ops, SparseCore 0:
  171.8 33.0 reduce-scatter.3
  267.1 31.4 reduce-scatter.5
  352.4 64.7 all-reduce.105
  419.7 33.8 reduce-scatter.7
  581.3 396.6 all-reduce.107
